TPU v7x, 512 devices: a whole 4x4x16 slice. The times are simulated.
512 devices in a mesh: row: 32 (over y_lo, z), col: 16 (over x, y_hi, core).
Axes of the slice: x: 4, y: 4 (y_hi: 2, y_lo: 2; y = y_hi * 2 + y_lo), z: 16, core: 2. Of those that a mesh axis runs over, the one named last changes fastest.
Arguments:
- anc_inverse: float32 [16384, 16384], P('row', 'col')
- panel: float32 [7680, 2560], P('row', 'col'), may hold values from -0.00390625 to 0.00390625
- local_rows: int32 [7680], P('row'), may hold values from -1 to 511, as said below
- inv_diag: float32 [2560, 2560], P('row', 'col')
Outputs:
- sigma_off: float32 [7680, 2560], P('row', 'col')
- sigma_diag: float32 [2560, 2560], P('row', 'col')
Inputs may be any that keep to these rules, and one draw needn't show every extreme that they name: `local_rows`: each aligned block of 240 slots lists its live ancestor rows first, distinct and ascending, then -1 in the rest; every block has at least one live slot, some block is full and some block is at most half full.
All inputs are finite; a program needn't handle non-finite values.
Results may differ from a plain program's by a relative error of at most 0.000075.
Values sent between devices are 32-bit elements; how exact they have to be, the bound alone decides.
A program may use at most 64 MiB of HBM per device.

v0:
```python
import jax
import jax.numpy as jnp
from jax import lax
from jax.sharding import PartitionSpec as P


def broadcast(value, axis, source):
    kept = jnp.where(lax.axis_index(axis) == source, value, 0).astype(value.dtype)
    return lax.psum(kept, axis)


def pick_columns(rows_sel, offset, width, lists):
    region = lax.slice_in_dim(rows_sel, offset, offset + width, axis=1)
    taken = jnp.take(region, jnp.maximum(lists, 0), axis=1)
    return taken * (lists >= 0).astype(jnp.float32)[None, :]


def shards(anc_inverse, panel, local_rows, inv_diag):
    anc_rows = anc_inverse.shape[0]
    groups = lax.axis_size("row") // lax.axis_size("col")
    col_index = lax.axis_index("col")
    own_live = (local_rows >= 0).astype(jnp.float32)
    rows_sel = jnp.take(anc_inverse, jnp.maximum(local_rows, 0), axis=0) * own_live[:, None]
    widened = lax.all_gather(panel, "col", axis=1, tiled=True)
    partial_sum = jnp.zeros(widened.shape, jnp.float32)
    for member in range(groups):
        root_index = col_index * groups + member
        block_panel, block_lists = (
            broadcast(widened, "row", root_index),
            broadcast(local_rows, "row", root_index),
        )
        square = pick_columns(rows_sel, member * anc_rows, anc_rows, block_lists)
        partial_sum = partial_sum - jnp.dot(square, block_panel, precision=lax.Precision.HIGHEST)
    sigma_off = lax.psum_scatter(partial_sum, "col", scatter_dimension=1, tiled=True)
    folded = lax.psum_scatter(
        lax.dot_general(
            widened, sigma_off, (((0,), (0,)), ((), ())), precision=lax.Precision.HIGHEST
        ),
        "row",
        scatter_dimension=0,
        tiled=True,
    )
    sigma_diag = inv_diag - folded
    return (sigma_off, sigma_diag)


def solution(mesh):
    placed = (P("row", "col"), P("row", "col"), P("row"), P("row", "col"))
    return jax.shard_map(
        shards,
        mesh=mesh,
        in_specs=placed,
        out_specs=(P("row", "col"), P("row", "col")),
        check_vma=False,
    )
```

profile of v0, /device:TPU:2, one launch (start us, length us, event | category | flops | bytes accessed | tf_op | source)
XLA Modules:
  0.0 619.5 jit_solution(7924383974669501724)
XLA Ops:
  7.2 0.0 copy-start
  7.2 0.0 all-gather.2.cloned.1.call-start
  7.2 0.7 all-gather.2.cloned.1.call-update
  7.9 0.0 all-reduce.4.cloned.1.call-start
  8.0 73.3 %all-gather.2.cloned.1.call-done = f32[240,2560]{0,1:T(8,128)} async-done(((f32[240,160]{0,1:T(8,128)}), f32[240,2560]{0,1:T(8,128)}) %all-gather.2.cloned.1.call-update) | async-done | bytes 2457616 | tf_op jit(solution)/shard_map/all_gather | solution.py:24
  81.3 4.4 broadcast_select_fusion
  85.7 0.0 copy-start.3
  85.7 0.0 all-reduce.4.cloned.1.call-update
  85.7 0.0 reduce-scatter.5.cloned.1.call-start
  85.8 0.6 copy-done.3
  86.4 0.0 copy-done
  86.4 1.0 gather_fusion
  87.5 0.2 select_multiply_fusion
  87.6 0.9 fusion.10
  88.5 0.2 copy.10
  88.7 1.2 copy.11
  89.9 24.0 %all-reduce = (s32[240]{0:T(256)S(1)}, s32[240]{0:T(256)S(1)}) all-reduce(s32[240]{0:T(256)S(1)} %get-tuple-element.21, s32[240]{0:T(256)S(1)} %get-tuple-element.19), channel_id=1, replica_groups=mesh['row'=32,'col'=16] {'row'}, use_global_device_ids=true, to_apply=%region_0.1 | all-reduce | flops 480 | bytes 3840 | tf_op jit(solution)/shard_map/psum | solution.py:9
  114.0 0.9 gather_fusion.1
  114.9 0.9 gather_fusion.2
  115.9 248.1 %all-reduce.4.cloned.1.call-done = (f32[240,2560]{0,1:T(8,128)}, f32[240,2560]{0,1:T(8,128)}) async-done(((f32[240,2560]{0,1:T(8,128)}, f32[240,2560]{0,1:T(8,128)}), (f32[240,2560]{0,1:T(8,128)}, f32[240,2560]{0,1:T(8,128)})) %all-reduce.4.cloned.1.call-update) | async-done | bytes 4915216 | tf_op jit(solution)/shard_map/psum | solution.py:9
  364.0 0.0 copy-start.1
  364.0 4.4 convolution_subtract_fusion.1
  368.5 0.0 copy-done.1
  368.5 4.0 convolution_subtract_fusion
  372.5 0.0 reduce-scatter.5.cloned.1.call-update
  372.5 0.0 reduce-scatter.7.cloned.1.call-start
  372.6 90.1 %reduce-scatter.5.cloned.1.call-done = f32[240,160]{0,1:T(8,128)} async-done(((f32[240,2560]{0,1:T(8,128)}), f32[240,160]{0,1:T(8,128)}) %reduce-scatter.5.cloned.1.call-update) | async-done | bytes 153616 | tf_op jit(solution)/shard_map/reduce_scatter | solution.py:34
  462.7 5.8 convolution_bitcast_fusion
  468.5 0.0 copy-start.2
  468.5 3.1 copy.14
  471.6 0.0 reduce-scatter.7.cloned.1.call-update
  471.6 0.0 copy-done.2
  471.6 0.1 copy.12
  471.7 139.5 %reduce-scatter.7.cloned.1.call-done = f32[80,160]{1,0:T(8,128)} async-done(((f32[2560,160]{1,0:T(8,128)}), f32[80,160]{1,0:T(8,128)}) %reduce-scatter.7.cloned.1.call-update) | async-done | bytes 51216
  611.2 1.0 copy.15
  612.2 0.7 copy.13
  (8 shorter events, 0.1 us)
Async XLA Ops:
  7.2 79.2 %copy-start = (f32[512,1024]{1,0:T(8,128)S(1)}, f32[512,1024]{1,0:T(8,128)}, u32[]{:S(2)}) copy-start(f32[512,1024]{1,0:T(8,128)} %param.6) | copy-start | bytes 6291460
  7.2 74.1 %all-gather.2.cloned.1.call-start = ((), (), s32[]{:S(2)}) async-start(), calls=%async_computation.2 | async-start | bytes 2785280 | tf_op jit(solution)/shard_map/all_gather | solution.py:24
  7.9 356.1 %all-reduce.4.cloned.1.call-start = ((), (), s32[]{:S(2)}) async-start(), calls=%async_computation.5 | async-start | bytes 10485760 | tf_op jit(solution)/shard_map/psum | solution.py:9
  85.7 0.7 copy-start.3
  85.7 377.0 %reduce-scatter.5.cloned.1.call-start = ((), (), s32[]{:S(2)}) async-start(), calls=%async_computation.3 | async-start | bytes 2785280 | tf_op jit(solution)/shard_map/reduce_scatter | solution.py:34
  364.0 4.5 copy-start.1
  372.5 238.7 %reduce-scatter.7.cloned.1.call-start = ((), (), s32[]{:S(2)}) async-start(), calls=%async_computation.4 | async-start | bytes 2703360
  468.5 3.1 copy-start.2
Sparse Core Ops, SparseCore 0:
  11.3 69.9 all-gather.1
  85.8 278.1 all-reduce.3
  372.6 89.9 reduce-scatter.4
  471.8 139.4 reduce-scatter.6
where the time goes:
time: 620 us; the launch traced here: 619 us
  waiting for transfers between devices  552 us (89%)
  blocking collectives  24 us (4%)
  matrix products  14.3 us (2%)
  between operations  13.9 us (2%)
  local copies, waits for them, and re-layouts  10.7 us (2%)
    psum x1, waiting for transfers between devices, broadcast(): return lax.psum(kept, axis)  248 us
    unnamed x5, waiting for transfers between devices  140 us
    reduce_scatter x1, waiting for transfers between devices, shards(): lax.psum_scatter(partial_sum, 'col', scatter_dimension=1, tiled=True)  90.1 us
    all_gather x1, waiting for transfers between devices, shards(): widened = lax.all_gather(panel, 'col', axis=1, tiled=True)  73.3 us
    psum x1, blocking collectives, broadcast(): return lax.psum(kept, axis)  24 us
  transfers between devices with their start and end apart: 4, of which 4 were waited for; matrix products, arithmetic and copies ran while one was open for 1% of the time, Pallas kernels for 0%

commit v1 on v0

v1 whole, which is shorter than its diff:
```python
import functools

import jax
import jax.numpy as jnp
from jax import lax
from jax.experimental import pallas as pl
from jax.experimental.pallas import tpu as pltpu
from jax.sharding import PartitionSpec as P

MESH = pl.DeviceIdType.MESH
Z = 16
SLOTS = 28
F32 = jnp.float32
BF16 = jnp.bfloat16


def split(value):
    high = value.astype(BF16)
    return high, (value - high.astype(F32)).astype(BF16)


def dot_nt(a, b):
    return lax.dot_general(a, b, (((1,), (1,)), ((), ())), preferred_element_type=F32)


def dot3(a, b):
    return dot_nt(a[0], b[0]) + (dot_nt(a[0], b[1]) + dot_nt(a[1], b[0]))


def remote(src, dst, send, recv, device):
    return pltpu.make_async_remote_copy(
        src_ref=src, dst_ref=dst, send_sem=send, recv_sem=recv, device_id=device, device_id_type=MESH
    )


def panel_kernel(
    xt, rows, lst, so, tp,
    XR, LB, CB, CH, CL, PB, RB, SG, XZ,
    xs, xr, asend, ls, lr, cs, cr, ds, dr, ss, sr, zs, zr, local,
):
    r, c = lax.axis_index("row"), lax.axis_index("col")
    yl, z = lax.div(r, Z), lax.rem(r, Z)
    k, p = lax.rem(c, 2), lax.div(c, 2)
    core = (r, c + 1 - 2 * k)
    across = (lax.rem(r + Z, 2 * Z), c)

    def at_z(step):
        return (Z * yl + lax.rem(z + step + Z, Z), c)

    up, down = at_z(1), at_z(-1)

    barrier = pltpu.get_barrier_semaphore()
    me = Z * yl + c

    @pl.loop(1, 32)
    def _(o):
        there = lax.rem(me + o, 32)
        pl.semaphore_signal(
            barrier, inc=1, device_id=(Z * lax.div(there, Z) + z, lax.rem(there, Z)), device_id_type=MESH
        )

    for there in (up, down):
        pl.semaphore_signal(barrier, inc=1, device_id=there, device_id_type=MESH)
    pl.semaphore_wait(barrier, 33)

    far = jnp.where(yl == lax.div(p, 4), 0, 1)

    def list_place(jj):
        return lax.rem(z - lax.rem(4 * p + 2 * k + jj, Z) + Z, Z)

    def list_slot(jj):
        e = list_place(jj)
        return jnp.minimum(e, Z - e) + far

    for jj in range(2):

        @pl.when((list_place(jj) == 0) & (far == 0))
        def _():
            pltpu.make_async_copy(lst, LB.at[jj], lr.at[jj]).start()

    def list_sends(jj):
        e = list_place(jj)
        return (
            (remote(LB.at[jj], LB.at[jj], ls.at[jj, 0], lr.at[jj], across), (e == 0) & (far == 0)),
            (remote(LB.at[jj], LB.at[jj], ls.at[jj, 1], lr.at[jj], up), e < 8),
            (remote(LB.at[jj], LB.at[jj], ls.at[jj, 2], lr.at[jj], down), (e == 0) | (e > 9)),
        )

    def list_step(jj):
        pltpu.make_async_copy(lst, LB.at[jj], lr.at[jj]).wait()
        for copy, wanted in list_sends(jj):
            pl.when(wanted)(copy.start)

    to_p, to_j, half_w = lax.div(r, 4), lax.rem(r, 4), lax.rem(p - lax.div(r, 4) + 8, 8)

    def own_send(h):
        return remote(
            xt.at[h], XR.at[to_j, half_w], asend.at[h], xr.at[to_j, half_w], (Z * h + z, 2 * to_p + k)
        )

    def own_local(h):
        return (to_p == p) & (yl == h)

    for jj in range(2):

        @pl.when(list_slot(jj) == 0)
        def _():
            list_step(jj)

    for h in range(2):

        @pl.when(own_local(h))
        def _():
            pltpu.make_async_copy(xt.at[h], XR.at[to_j, half_w], xr.at[to_j, half_w]).start()

        @pl.when(jnp.logical_not(own_local(h)))
        def _():
            own_send(h).start()

    base = lax.rem(4 * p, Z)
    u = lax.rem(z - base + Z, Z)
    v = lax.rem(base + 3 - z + Z, Z)

    def ring(j, w, there):
        return remote(XR.at[j, w], XR.at[j, w], xs.at[j, w], xr.at[j, w], there)

    def forward(s, place, way, odd):
        low, late = jnp.minimum(place, 3), jnp.maximum(place - 3, 0)

        def step(t, j, d):
            w = 2 * lax.div(t, 4) + odd
            copy = ring(3 - j if odd else j, w, way)
            copy.wait_recv()
            pl.when(d < 15)(copy.start)

        t = jnp.maximum(s - late, 0)
        i = lax.rem(t, 4)

        @pl.when((s >= late) & (t < 16) & (i <= low))
        def _():
            step(t, low - i, late + i)

        t2 = jnp.maximum(s - 12, 0)
        i2 = lax.rem(t2, 4)

        @pl.when((s >= 12) & (t2 < 16) & (i2 > low))
        def _():
            step(t2, low - i2 + 4, 12 + i2)

    tile, tile_half = lax.rem(c, 8), lax.div(c, 8)

    def plane_send(o):
        there = lax.rem(c + o, 16)
        return remote(
            xt.at[:, lax.rem(there, 2)], XZ.at[yl, tile], zs.at[o], zr.at[yl, tile], (Z * tile_half + z, there)
        )

    plane_self = tile_half == yl

    @pl.when(plane_self)
    def _():
        pltpu.make_async_copy(xt.at[:, k], XZ.at[yl, tile], zr.at[yl, tile]).start()

    def c_core():
        return remote(CB.at[yl, k], CB.at[yl, k], cs.at[0], cr.at[0], core)

    def c_across():
        return remote(CB.at[yl, k], CB.at[yl, k], cs.at[1], cr.at[1], across)

    def c_relay():
        return remote(CB.at[1 - yl, k], CB.at[1 - yl, k], cs.at[2], cr.at[2], core)

    pick_slot = jnp.maximum(list_slot(0), list_slot(1)) + 1

    def pick():
        for jj in range(2):
            hit = lax.broadcasted_iota(jnp.int32, (512, 256), 0).astype(F32) == LB[jj, 0:1, :]
            hit = jnp.where(hit, 1.0, 0.0).astype(BF16)
            block = rows[:, 512 * jj : 512 * jj + 512]
            high, mid = split(block)
            rest = ((block - high.astype(F32)) - mid.astype(F32)).astype(BF16)
            parts = [jnp.dot(x, hit, preferred_element_type=F32) for x in (high, mid, rest)]
            CB[yl, k, jj] = parts[0] + (parts[1] + parts[2])
        c_across().start()
        c_core().start()

    @pl.loop(0, SLOTS)
    def _(s):
        for jj in range(2):

            @pl.when((s > 0) & (list_slot(jj) == s))
            def _():
                list_step(jj)

        forward(s, u, up, 0)
        forward(s, v, down, 1)

        @pl.when(s == pick_slot)
        def _():
            pick()

        @pl.when(s == pick_slot + 8)
        def _():
            c_across().wait_recv()
            c_relay().start()

        @pl.when((s >= 4) & (s < 20) & jnp.logical_not(plane_self & (s == 4)))
        def _():
            plane_send(s - 4).start()

    c_core().wait_recv()
    c_relay().wait_recv()
    for yb in range(2):
        for j in range(4):
            high, low = split(CB[yb, j // 2, j % 2])
            CH[yb, j], CL[yb, j] = high, low

    def peer(w):
        return remote(PB.at[w], RB.at[w], ds.at[w], dr.at[w], (r, 2 * lax.rem(p + w, 8) + k))

    @pl.loop(0, 8)
    def _(o):
        w = 7 - o
        pieces = [split(XR[j, w].reshape(80, 256)) for j in range(4)]
        for yb in range(2):
            total = jnp.zeros((80, 256), F32)
            for j in range(4):
                total = total + dot3(pieces[j], (CH[yb, j], CL[yb, j]))
            PB[w, :, 256 * yb : 256 * yb + 256] = total

        @pl.when(w > 0)
        def _():
            peer(w).start()

    total = PB[0]
    for w in range(1, 8):
        peer(w).wait_recv()
        total = total + RB[w]
    SG[k, yl] = -total

    def s_across():
        return remote(SG.at[k, yl], SG.at[k, yl], ss.at[0], sr.at[0], across)

    def s_core():
        return remote(SG.at[k, yl], SG.at[k, yl], ss.at[1], sr.at[1], core)

    def s_relay():
        return remote(SG.at[k, 1 - yl], SG.at[k, 1 - yl], ss.at[2], sr.at[2], core)

    s_across().start()
    s_core().start()
    s_across().wait_recv()
    s_relay().start()
    so[...] = SG[k, :, :, pl.ds(pl.multiple_of(256 * yl, 256), 256)]
    s_core().wait_recv()
    s_relay().wait_recv()

    for i in range(16):
        pltpu.make_async_copy(xt.at[:, 0], XZ.at[i // 8, i % 8], zr.at[i // 8, i % 8]).wait()
    sides = [split(SG[:, :, :, 256 * yb : 256 * yb + 256].reshape(320, 256)) for yb in range(2)]

    @pl.loop(0, 8)
    def _(t):
        total = jnp.zeros((80, 320), F32)
        for yb in range(2):
            total = total + dot3(split(XZ[yb, t].reshape(80, 256)), sides[yb])
        tp[pl.ds(2 * t, 2), :, 0:320] = total.reshape(2, 40, 320)

    for jj in range(2):
        for copy, wanted in list_sends(jj):
            pl.when(wanted)(copy.wait_send)
    for h in range(2):
        pl.when(jnp.logical_not(own_local(h)))(own_send(h).wait_send)

    @pl.loop(0, 16)
    def _(n):
        j, q = lax.div(n, 4), lax.rem(n, 4)
        pl.when(lax.rem(u - j + Z, Z) < 15)(ring(j, 2 * q, up).wait_send)
        pl.when(lax.rem(v - 3 + j + Z, Z) < 15)(ring(j, 2 * q + 1, down).wait_send)
        pl.when(jnp.logical_not(plane_self & (n == 0)))(plane_send(n).wait_send)

    for copy in (c_core(), c_across(), c_relay(), s_across(), s_core(), s_relay()):
        copy.wait_send()

    @pl.loop(1, 8)
    def _(w):
        peer(w).wait_send()


def fold_kernel(tp, inv, out, SU, RU, SD, RD, PX, su, ru, sd, rd, px):
    r, c = lax.axis_index("row"), lax.axis_index("col")
    yl, z, k = lax.div(r, Z), lax.rem(r, Z), lax.rem(c, 2)
    core = (r, c + 1 - 2 * k)

    def at_z(step):
        return (Z * yl + lax.rem(z + step + Z, Z), c)

    barrier = pltpu.get_barrier_semaphore()
    for there in (at_z(1), at_z(-1), core):
        pl.semaphore_signal(barrier, inc=1, device_id=there, device_id_type=MESH)
    pl.semaphore_wait(barrier, 3)

    def up(s):
        return remote(SU.at[s], RU.at[s], su.at[s], ru.at[s], at_z(1))

    def down(s):
        return remote(SD.at[s], RD.at[s], sd.at[s], rd.at[s], at_z(-1))

    for s in range(8):
        mine = tp[lax.rem(z + 8 - s, Z)]
        if s:
            up(s - 1).wait_recv()
            mine = mine + RU[s - 1]
        SU[s] = mine
        up(s).start()
        if s < 7:
            mine = tp[lax.rem(z + 9 + s, Z)]
            if s:
                down(s - 1).wait_recv()
                mine = mine + RD[s - 1]
            SD[s] = mine
            down(s).start()
    down(6).wait_recv()
    mine = tp[z] + RD[6]
    up(7).wait_recv()
    PX[0] = mine + RU[7]
    swap = remote(PX.at[0], PX.at[1], px.at[0], px.at[1], core)
    swap.start()
    swap.wait_recv()
    own, other = PX[0], PX[1]
    own = jnp.where(k == 0, own[:, 0:160], own[:, 160:320])
    other = jnp.where(k == 0, other[:, 0:160], other[:, 160:320])
    out[0:40, :] = inv[0:40, :] - jnp.where(k == 0, own, other)
    out[40:80, :] = inv[40:80, :] - jnp.where(k == 0, other, own)
    swap.wait_send()
    for s in range(8):
        up(s).wait_send()
        if s < 7:
            down(s).wait_send()


def shards(anc_inverse, panel, local_rows, inv_diag):
    ids = jnp.pad(local_rows, (0, 16), constant_values=-1)
    live = (ids >= 0).astype(F32)
    rows = jnp.take(anc_inverse, jnp.maximum(ids, 0), axis=0) * live[:, None]
    lst = jnp.broadcast_to(ids.astype(F32)[None, :], (8, 256))
    xt = jnp.pad(panel, ((0, 16), (0, 0))).T.reshape(2, 2, 40, 256)
    vmem = pl.BlockSpec(memory_space=pltpu.VMEM)
    dma = pltpu.SemaphoreType.DMA
    so, tp = pl.pallas_call(
        panel_kernel,
        out_shape=(
            jax.ShapeDtypeStruct((2, 80, 256), F32),
            jax.ShapeDtypeStruct((Z, 40, 384), F32),
        ),
        in_specs=[vmem] * 3,
        out_specs=(vmem, vmem),
        scratch_shapes=[
            pltpu.VMEM((4, 8, 2, 40, 256), F32),
            pltpu.VMEM((2, 8, 256), F32),
            pltpu.VMEM((2, 2, 2, 256, 256), F32),
            pltpu.VMEM((2, 4, 256, 256), BF16),
            pltpu.VMEM((2, 4, 256, 256), BF16),
            pltpu.VMEM((8, 80, 512), F32),
            pltpu.VMEM((8, 80, 512), F32),
            pltpu.VMEM((2, 2, 80, 512), F32),
            pltpu.VMEM((2, 8, 2, 40, 256), F32),
            dma((4, 8)), dma((4, 8)),
            dma((2,)),
            dma((2, 3)), dma((2,)),
            dma((3,)), dma((3,)),
            dma((8,)), dma((8,)),
            dma((3,)), dma((3,)),
            dma((16,)), dma((2, 8)),
            dma((2,)),
        ],
        compiler_params=pltpu.CompilerParams(collective_id=0, has_side_effects=True),
        name="panel_products",
    )(xt, rows, lst)
    sigma_diag = pl.pallas_call(
        fold_kernel,
        out_shape=jax.ShapeDtypeStruct(inv_diag.shape, F32),
        in_specs=[vmem] * 2,
        out_specs=vmem,
        scratch_shapes=[pltpu.VMEM((8, 40, 384), F32)] * 4
        + [pltpu.VMEM((2, 40, 384), F32)]
        + [dma((8,))] * 4
        + [dma((2,))],
        compiler_params=pltpu.CompilerParams(collective_id=1, has_side_effects=True),
        name="fold_over_rows",
    )(tp, inv_diag)
    sigma_off = so.reshape(160, 256)[:, :240].T
    return (sigma_off, sigma_diag)


def solution(mesh):
    placed = (P("row", "col"), P("row", "col"), P("row"), P("row", "col"))
    return jax.shard_map(
        shards,
        mesh=mesh,
        in_specs=placed,
        out_specs=(P("row", "col"), P("row", "col")),
        check_vma=False,
    )
```

time: 620 us -> 195 us (0.31)
  the two profiles are of different devices: /device:TPU:2 before, /device:TPU:7 now
where the time goes in v1:
time: 195 us; the launch traced here: 191 us
  Pallas kernels  181 us (93%)
  local copies, waits for them, and re-layouts  6.39 us (3%)
  other arithmetic  2.67 us (1%)
    pallas_call x1, Pallas kernels, shards(): pl.pallas_call(panel_kernel, out_shape=(jax.ShapeDtypeStruct((2, 80, 256)...  150 us
    pallas_call x1, Pallas kernels, shards(): pl.pallas_call(fold_kernel, out_shape=jax.ShapeDtypeStruct(inv_diag.shape...  31.1 us

profile of v1, /device:TPU:7, one launch (start us, length us, event | category | flops | bytes accessed | tf_op | source)
XLA Modules:
  0.0 190.7 jit_solution(8784400476603361705)
XLA Ops:
  0.6 0.0 copy-start
  0.6 0.8 broadcast_compare_fusion
  1.5 0.7 pad_convert_fusion
  2.2 0.6 broadcast_in_dim.22.lst
  2.8 1.6 pad.8
  4.4 0.0 copy-done
  4.4 1.1 gather_fusion
  5.4 1.1 select_multiply_fusion.rows
  6.6 149.9 %panel_products.1 = (f32[2,80,256]{2,1,0:T(8,128)}, f32[16,40,384]{2,1,0:T(8,128)}) custom-call(f32[2,2,40,256]{3,2,1,0:T(8,128)} %bitcast.6, f32[256,1024]{1,0:T(8,128)} %select_multiply_fusion.rows, f32[8,256]{1,0:T(8,128)} %broadcast_in_dim.22.lst), custom_call_target="tpu_custom_call" | custom-call | tf_op jit(solution)/shard_map/panel_products/pallas_call | solution.py:350
  156.5 1.6 slice_bitcast_fusion
  158.1 31.1 %fold_over_rows.1 = f32[80,160]{1,0:T(8,128)} custom-call(f32[16,40,384]{2,1,0:T(8,128)} %get-tuple-element.5.tp, f32[80,160]{1,0:T(8,128)} %inv.1), custom_call_target="tpu_custom_call" | custom-call | tf_op jit(solution)/shard_map/fold_over_rows/pallas_call | solution.py:380
  189.2 1.5 copy.7
  (1 shorter events, 0.0 us)
Async XLA Ops:
  0.6 3.7 %copy-start = (f32[512,1024]{1,0:T(8,128)S(1)}, f32[512,1024]{1,0:T(8,128)}, u32[]{:S(2)}) copy-start(f32[512,1024]{1,0:T(8,128)} %param.4) | copy-start | bytes 6291460

commit v2 on v1

--- a/solution.py
+++ b/solution.py
@@ -9,7 +9,12 @@
 
 MESH = pl.DeviceIdType.MESH
 Z = 16
-SLOTS = 28
+PARTS = 1
+PIECE = 80 // PARTS
+HOP = 1
+C_RELAY = 6
+C_READY = 9
+GROUPS = max(8 * PARTS + 3 + 12 * HOP, 10 + C_READY + 7 * PARTS) + 2
 F32 = jnp.float32
 BF16 = jnp.bfloat16
 
@@ -36,7 +41,7 @@
 def panel_kernel(
     xt, rows, lst, so, tp,
     XR, LB, CB, CH, CL, PB, RB, SG, XZ,
-    xs, xr, asend, ls, lr, cs, cr, ds, dr, ss, sr, zs, zr, local,
+    xs, xr, asend, ls, lr, cs, cr, ds, dr, ss, sr, zs, zr,
 ):
     r, c = lax.axis_index("row"), lax.axis_index("col")
     yl, z = lax.div(r, Z), lax.rem(r, Z)
@@ -93,10 +98,13 @@
 
     to_p, to_j, half_w = lax.div(r, 4), lax.rem(r, 4), lax.rem(p - lax.div(r, 4) + 8, 8)
 
-    def own_send(h):
-        return remote(
-            xt.at[h], XR.at[to_j, half_w], asend.at[h], xr.at[to_j, half_w], (Z * h + z, 2 * to_p + k)
-        )
+    def own_pair(h, part):
+        there = XR.at[to_j, half_w, pl.ds(PIECE * part, PIECE)]
+        return xt.at[h, pl.ds(PIECE * part, PIECE)], there, xr.at[to_j, PARTS * half_w + part]
+
+    def own_send(h, part):
+        src, dst, sem = own_pair(h, part)
+        return remote(src, dst, asend.at[h, part], sem, (Z * h + z, 2 * to_p + k))
 
     def own_local(h):
         return (to_p == p) & (yl == h)
@@ -107,59 +115,56 @@
         def _():
             list_step(jj)
 
-    for h in range(2):
-
-        @pl.when(own_local(h))
-        def _():
-            pltpu.make_async_copy(xt.at[h], XR.at[to_j, half_w], xr.at[to_j, half_w]).start()
-
-        @pl.when(jnp.logical_not(own_local(h)))
-        def _():
-            own_send(h).start()
+    for part in range(PARTS):
+        for h in range(2):
+
+            @pl.when(own_local(h))
+            def _():
+                pltpu.make_async_copy(*own_pair(h, part)).start()
+
+            @pl.when(jnp.logical_not(own_local(h)))
+            def _():
+                own_send(h, part).start()
 
     base = lax.rem(4 * p, Z)
-    u = lax.rem(z - base + Z, Z)
-    v = lax.rem(base + 3 - z + Z, Z)
-
-    def ring(j, w, there):
-        return remote(XR.at[j, w], XR.at[j, w], xs.at[j, w], xr.at[j, w], there)
-
-    def forward(s, place, way, odd):
-        low, late = jnp.minimum(place, 3), jnp.maximum(place - 3, 0)
-
-        def step(t, j, d):
-            w = 2 * lax.div(t, 4) + odd
-            copy = ring(3 - j if odd else j, w, way)
+    place = jnp.where(k == 0, lax.rem(z - base + Z, Z), lax.rem(base + 3 - z + Z, Z))
+    low, late = jnp.minimum(place, 3), jnp.maximum(place - 3, 0)
+    onward = at_z(1 - 2 * k)
+
+    def ring(j, n):
+        w, part = lax.div(n, PARTS), lax.rem(n, PARTS)
+        piece = XR.at[j, w, pl.ds(PIECE * part, PIECE)]
+        return remote(piece, piece, xs.at[j, n], xr.at[j, n], onward)
+
+    def behind(i):
+        return jnp.where(i <= low, late, 12)
+
+    def line_block(i):
+        line = jnp.where(i <= low, low - i, low - i + 4)
+        return jnp.where(k == 0, line, 3 - line)
+
+    def forward(g, i):
+        n = g - HOP * behind(i) - i
+
+        @pl.when((n >= 0) & (n < 8 * PARTS))
+        def _():
+            copy = ring(line_block(i), jnp.maximum(n, 0))
             copy.wait_recv()
-            pl.when(d < 15)(copy.start)
-
-        t = jnp.maximum(s - late, 0)
-        i = lax.rem(t, 4)
-
-        @pl.when((s >= late) & (t < 16) & (i <= low))
-        def _():
-            step(t, low - i, late + i)
-
-        t2 = jnp.maximum(s - 12, 0)
-        i2 = lax.rem(t2, 4)
-
-        @pl.when((s >= 12) & (t2 < 16) & (i2 > low))
-        def _():
-            step(t2, low - i2 + 4, 12 + i2)
+            pl.when(behind(i) + i < 15)(copy.start)
 
     tile, tile_half = lax.rem(c, 8), lax.div(c, 8)
 
     def plane_send(o):
         there = lax.rem(c + o, 16)
         return remote(
-            xt.at[:, lax.rem(there, 2)], XZ.at[yl, tile], zs.at[o], zr.at[yl, tile], (Z * tile_half + z, there)
+            xt.at[:, pl.ds(40 * lax.rem(there, 2), 40)], XZ.at[yl, tile], zs.at[o], zr.at[yl, tile], (Z * tile_half + z, there)
         )
 
     plane_self = tile_half == yl
 
     @pl.when(plane_self)
     def _():
-        pltpu.make_async_copy(xt.at[:, k], XZ.at[yl, tile], zr.at[yl, tile]).start()
+        pltpu.make_async_copy(xt.at[:, pl.ds(40 * k, 40)], XZ.at[yl, tile], zr.at[yl, tile]).start()
 
     def c_core():
         return remote(CB.at[yl, k], CB.at[yl, k], cs.at[0], cr.at[0], core)
@@ -171,6 +176,7 @@
         return remote(CB.at[1 - yl, k], CB.at[1 - yl, k], cs.at[2], cr.at[2], core)
 
     pick_slot = jnp.maximum(list_slot(0), list_slot(1)) + 1
+    c_slot = pick_slot + C_READY
 
     def pick():
         for jj in range(2):
@@ -184,44 +190,19 @@
         c_across().start()
         c_core().start()
 
-    @pl.loop(0, SLOTS)
-    def _(s):
-        for jj in range(2):
-
-            @pl.when((s > 0) & (list_slot(jj) == s))
-            def _():
-                list_step(jj)
-
-        forward(s, u, up, 0)
-        forward(s, v, down, 1)
-
-        @pl.when(s == pick_slot)
-        def _():
-            pick()
-
-        @pl.when(s == pick_slot + 8)
-        def _():
-            c_across().wait_recv()
-            c_relay().start()
-
-        @pl.when((s >= 4) & (s < 20) & jnp.logical_not(plane_self & (s == 4)))
-        def _():
-            plane_send(s - 4).start()
-
-    c_core().wait_recv()
-    c_relay().wait_recv()
-    for yb in range(2):
-        for j in range(4):
-            high, low = split(CB[yb, j // 2, j % 2])
-            CH[yb, j], CL[yb, j] = high, low
+    def c_arrived():
+        c_core().wait_recv()
+        c_relay().wait_recv()
+        for yb in range(2):
+            for j in range(4):
+                high, low = split(CB[yb, j // 2, j % 2])
+                CH[yb, j], CL[yb, j] = high, low
 
     def peer(w):
         return remote(PB.at[w], RB.at[w], ds.at[w], dr.at[w], (r, 2 * lax.rem(p + w, 8) + k))
 
-    @pl.loop(0, 8)
-    def _(o):
-        w = 7 - o
-        pieces = [split(XR[j, w].reshape(80, 256)) for j in range(4)]
+    def multiply(w):
+        pieces = [split(XR[j, w]) for j in range(4)]
         for yb in range(2):
             total = jnp.zeros((80, 256), F32)
             for j in range(4):
@@ -231,6 +212,37 @@
         @pl.when(w > 0)
         def _():
             peer(w).start()
+
+    first_multiply = jnp.maximum(PARTS + 3 + HOP * behind(3), c_slot)
+
+    @pl.loop(0, GROUPS)
+    def _(g):
+        for jj in range(2):
+
+            @pl.when((g > 0) & (list_slot(jj) == g))
+            def _():
+                list_step(jj)
+
+        for i in range(4):
+            forward(g, i)
+
+        pl.when(g == pick_slot)(pick)
+
+        @pl.when(g == pick_slot + C_RELAY)
+        def _():
+            c_across().wait_recv()
+            c_relay().start()
+
+        @pl.when((g >= 1) & (g <= 16) & jnp.logical_not(plane_self & (g == 1)))
+        def _():
+            plane_send(g - 1).start()
+
+        pl.when(g == c_slot)(c_arrived)
+        ready = g - first_multiply
+
+        @pl.when((ready >= 0) & (ready < 8 * PARTS) & (lax.rem(jnp.maximum(ready, 0), PARTS) == 0))
+        def _():
+            multiply(lax.div(ready, PARTS))
 
     total = PB[0]
     for w in range(1, 8):
@@ -256,7 +268,7 @@
     s_relay().wait_recv()
 
     for i in range(16):
-        pltpu.make_async_copy(xt.at[:, 0], XZ.at[i // 8, i % 8], zr.at[i // 8, i % 8]).wait()
+        pltpu.make_async_copy(xt.at[:, pl.ds(0, 40)], XZ.at[i // 8, i % 8], zr.at[i // 8, i % 8]).wait()
     sides = [split(SG[:, :, :, 256 * yb : 256 * yb + 256].reshape(320, 256)) for yb in range(2)]
 
     @pl.loop(0, 8)
@@ -270,14 +282,20 @@
         for copy, wanted in list_sends(jj):
             pl.when(wanted)(copy.wait_send)
     for h in range(2):
-        pl.when(jnp.logical_not(own_local(h)))(own_send(h).wait_send)
+        for part in range(PARTS):
+            pl.when(jnp.logical_not(own_local(h)))(own_send(h, part).wait_send)
 
     @pl.loop(0, 16)
     def _(n):
-        j, q = lax.div(n, 4), lax.rem(n, 4)
-        pl.when(lax.rem(u - j + Z, Z) < 15)(ring(j, 2 * q, up).wait_send)
-        pl.when(lax.rem(v - 3 + j + Z, Z) < 15)(ring(j, 2 * q + 1, down).wait_send)
         pl.when(jnp.logical_not(plane_self & (n == 0)))(plane_send(n).wait_send)
+
+    for i in range(4):
+
+        @pl.when(behind(i) + i < 15)
+        def _():
+            @pl.loop(0, 8 * PARTS)
+            def _(n):
+                ring(line_block(i), n).wait_send()
 
     for copy in (c_core(), c_across(), c_relay(), s_across(), s_core(), s_relay()):
         copy.wait_send()
@@ -344,7 +362,7 @@
     live = (ids >= 0).astype(F32)
     rows = jnp.take(anc_inverse, jnp.maximum(ids, 0), axis=0) * live[:, None]
     lst = jnp.broadcast_to(ids.astype(F32)[None, :], (8, 256))
-    xt = jnp.pad(panel, ((0, 16), (0, 0))).T.reshape(2, 2, 40, 256)
+    xt = jnp.pad(panel, ((0, 16), (0, 0))).T.reshape(2, 80, 256)
     vmem = pl.BlockSpec(memory_space=pltpu.VMEM)
     dma = pltpu.SemaphoreType.DMA
     so, tp = pl.pallas_call(
@@ -356,7 +374,7 @@
         in_specs=[vmem] * 3,
         out_specs=(vmem, vmem),
         scratch_shapes=[
-            pltpu.VMEM((4, 8, 2, 40, 256), F32),
+            pltpu.VMEM((4, 8, 80, 256), F32),
             pltpu.VMEM((2, 8, 256), F32),
             pltpu.VMEM((2, 2, 2, 256, 256), F32),
             pltpu.VMEM((2, 4, 256, 256), BF16),
@@ -365,14 +383,13 @@
             pltpu.VMEM((8, 80, 512), F32),
             pltpu.VMEM((2, 2, 80, 512), F32),
             pltpu.VMEM((2, 8, 2, 40, 256), F32),
-            dma((4, 8)), dma((4, 8)),
-            dma((2,)),
+            dma((4, 8 * PARTS)), dma((4, 8 * PARTS)),
+            dma((2, PARTS)),
             dma((2, 3)), dma((2,)),
             dma((3,)), dma((3,)),
             dma((8,)), dma((8,)),
             dma((3,)), dma((3,)),
             dma((16,)), dma((2, 8)),
-            dma((2,)),
         ],
         compiler_params=pltpu.CompilerParams(collective_id=0, has_side_effects=True),
         name="panel_products",

time: 195 us -> 166 us (0.85)
  the two profiles are of different devices: /device:TPU:7 before, /device:TPU:21 now
where the time goes in v2:
time: 166 us; the launch traced here: 165 us
  Pallas kernels  156 us (94%)
  local copies, waits for them, and re-layouts  6.39 us (4%)
  other arithmetic  2.67 us (2%)
    pallas_call x1, Pallas kernels, shards(): pl.pallas_call(panel_kernel, out_shape=(jax.ShapeDtypeStruct((2, 80, 256)...  112 us
    pallas_call x1, Pallas kernels, shards(): pl.pallas_call(fold_kernel, out_shape=jax.ShapeDtypeStruct(inv_diag.shape...  43.5 us

profile of v2, /device:TPU:21, one launch (start us, length us, event | category | flops | bytes accessed | tf_op | source)
XLA Modules:
  0.0 165.5 jit_solution(11173209561881701545)
XLA Ops:
  0.6 0.0 copy-start
  0.6 0.8 broadcast_compare_fusion
  1.5 0.7 pad_convert_fusion
  2.2 0.6 broadcast_in_dim.22.lst
  2.8 1.6 pad.8
  4.4 0.0 copy-done
  4.4 1.1 gather_fusion
  5.4 1.1 select_multiply_fusion.rows
  6.6 112.2 %panel_products.1 = (f32[2,80,256]{2,1,0:T(8,128)}, f32[16,40,384]{2,1,0:T(8,128)}) custom-call(f32[2,80,256]{2,1,0:T(8,128)} %bitcast.6, f32[256,1024]{1,0:T(8,128)} %select_multiply_fusion.rows, f32[8,256]{1,0:T(8,128)} %broadcast_in_dim.22.lst), custom_call_target="tpu_custom_call" | custom-call | tf_op jit(solution)/shard_map/panel_products/pallas_call | solution.py:368
  118.8 1.6 slice_bitcast_fusion
  120.4 43.5 %fold_over_rows.1 = f32[80,160]{1,0:T(8,128)} custom-call(f32[16,40,384]{2,1,0:T(8,128)} %get-tuple-element.5.tp, f32[80,160]{1,0:T(8,128)} %inv.1), custom_call_target="tpu_custom_call" | custom-call | tf_op jit(solution)/shard_map/fold_over_rows/pallas_call | solution.py:397
  163.9 1.5 copy.7
  (1 shorter events, 0.0 us)
Async XLA Ops:
  0.6 3.7 %copy-start = (f32[512,1024]{1,0:T(8,128)S(1)}, f32[512,1024]{1,0:T(8,128)}, u32[]{:S(2)}) copy-start(f32[512,1024]{1,0:T(8,128)} %param.4) | copy-start | bytes 6291460

commit v3 on v2

v3 whole, which is shorter than its diff:
```python
import functools

import jax
import jax.numpy as jnp
from jax import lax
from jax.experimental import pallas as pl
from jax.experimental.pallas import tpu as pltpu
from jax.sharding import PartitionSpec as P

MESH = pl.DeviceIdType.MESH
Z = 16
PARTS = 1
PIECE = 80 // PARTS
HOP = 1
C_RELAY = 4
C_READY = 6
GROUPS = max(8 * PARTS + 3 + 12 * HOP, 10 + C_READY + 7 * PARTS) + 2
FOLDS = ((0, 24), (24, 16))
F32 = jnp.float32
BF16 = jnp.bfloat16


def split(value):
    high = value.astype(BF16)
    return high, (value - high.astype(F32)).astype(BF16)


def dot_nt(a, b):
    return lax.dot_general(a, b, (((1,), (1,)), ((), ())), preferred_element_type=F32)


def dot3(a, b):
    count = a.shape[0] // 2
    both = dot_nt(a, b[0])
    return both[:count] + (both[count:] + dot_nt(a[:count], b[1]))


def stack(value):
    return jnp.concatenate(split(value), axis=0)


def remote(src, dst, send, recv, device):
    return pltpu.make_async_remote_copy(
        src_ref=src, dst_ref=dst, send_sem=send, recv_sem=recv, device_id=device, device_id_type=MESH
    )


def panel_kernel(
    anc, panel, ids, so, diag,
    AV, xt, lst, XR, LB, CB, CH, CL, PB, RB, SG, XZ, tp, FS, FR, PX,
    xs, xr, asend, ls, lr, cs, cr, ds, dr, ss, sr, zs, zr, av, fs, fr, px,
):
    r, c = lax.axis_index("row"), lax.axis_index("col")
    yl, z = lax.div(r, Z), lax.rem(r, Z)
    k, p = lax.rem(c, 2), lax.div(c, 2)
    core = (r, c + 1 - 2 * k)
    across = (lax.rem(r + Z, 2 * Z), c)

    take_anc = pltpu.make_async_copy(anc, AV, av)
    take_anc.start()
    xt[...] = jnp.zeros_like(xt)
    xt[:, :, 0:240] = panel[...].reshape(2, 80, 240)
    lst[...] = jnp.full_like(lst, -1.0)
    lst[:, 0:240] = jnp.broadcast_to(ids[...].astype(F32), (8, 240))

    def at_z(step):
        return (Z * yl + lax.rem(z + step + Z, Z), c)

    up, down = at_z(1), at_z(-1)

    barrier = pltpu.get_barrier_semaphore()
    me = Z * yl + c

    @pl.loop(1, 32)
    def _(o):
        there = lax.rem(me + o, 32)
        pl.semaphore_signal(
            barrier, inc=1, device_id=(Z * lax.div(there, Z) + z, lax.rem(there, Z)), device_id_type=MESH
        )

    for there in (up, down, at_z(5), at_z(-5)):
        pl.semaphore_signal(barrier, inc=1, device_id=there, device_id_type=MESH)
    pl.semaphore_wait(barrier, 35)

    far = jnp.where(yl == lax.div(p, 4), 0, 1)

    def list_place(jj):
        return lax.rem(z - lax.rem(4 * p + 2 * k + jj, Z) + Z, Z)

    def list_slot(jj):
        e = list_place(jj)
        return jnp.minimum(e, Z - e) + far

    for jj in range(2):

        @pl.when((list_place(jj) == 0) & (far == 0))
        def _():
            pltpu.make_async_copy(lst, LB.at[jj], lr.at[jj]).start()

    def list_sends(jj):
        e = list_place(jj)
        return (
            (remote(LB.at[jj], LB.at[jj], ls.at[jj, 0], lr.at[jj], across), (e == 0) & (far == 0)),
            (remote(LB.at[jj], LB.at[jj], ls.at[jj, 1], lr.at[jj], up), e < 8),
            (remote(LB.at[jj], LB.at[jj], ls.at[jj, 2], lr.at[jj], down), (e == 0) | (e > 9)),
        )

    def list_step(jj):
        pltpu.make_async_copy(lst, LB.at[jj], lr.at[jj]).wait()
        for copy, wanted in list_sends(jj):
            pl.when(wanted)(copy.start)

    to_p, to_j = lax.div(r, 4), lax.rem(r, 4)
    turn = 4 * lax.rem(p + to_p, 2) + lax.rem(lax.div(p, 2) - lax.div(to_p, 2) + 4, 4)
    own_n = lax.rem(8 - turn, 8)

    def own_pair(h, part):
        there = XR.at[to_j, own_n, pl.ds(PIECE * part, PIECE)]
        return xt.at[h, pl.ds(PIECE * part, PIECE)], there, xr.at[to_j, PARTS * own_n + part]

    def own_send(h, part):
        src, dst, sem = own_pair(h, part)
        return remote(src, dst, asend.at[h, part], sem, (Z * h + z, 2 * to_p + k))

    def own_local(h):
        return (to_p == p) & (yl == h)

    for jj in range(2):

        @pl.when(list_slot(jj) == 0)
        def _():
            list_step(jj)

    for part in range(PARTS):
        for h in range(2):

            @pl.when(own_local(h))
            def _():
                pltpu.make_async_copy(*own_pair(h, part)).start()

            @pl.when(jnp.logical_not(own_local(h)))
            def _():
                own_send(h, part).start()

    base = lax.rem(4 * p, Z)
    place = jnp.where(k == 0, lax.rem(z - base + Z, Z), lax.rem(base + 3 - z + Z, Z))
    low, late = jnp.minimum(place, 3), jnp.maximum(place - 3, 0)
    onward = at_z(1 - 2 * k)

    def ring(j, n):
        w, part = lax.div(n, PARTS), lax.rem(n, PARTS)
        piece = XR.at[j, w, pl.ds(PIECE * part, PIECE)]
        return remote(piece, piece, xs.at[j, n], xr.at[j, n], onward)

    def behind(i):
        return jnp.where(i <= low, late, 12)

    def line_block(i):
        line = jnp.where(i <= low, low - i, low - i + 4)
        return jnp.where(k == 0, line, 3 - line)

    def forward(g, i):
        n = g - HOP * behind(i) - i

        @pl.when((n >= 0) & (n < 8 * PARTS))
        def _():
            copy = ring(line_block(i), jnp.maximum(n, 0))
            copy.wait_recv()
            pl.when(behind(i) + i < 15)(copy.start)

    tile, tile_half = lax.rem(c, 8), lax.div(c, 8)

    def plane_send(o):
        there = lax.rem(c + o, 16)
        return remote(
            xt.at[:, pl.ds(40 * lax.rem(there, 2), 40)], XZ.at[yl, tile], zs.at[o], zr.at[yl, tile], (Z * tile_half + z, there)
        )

    plane_self = tile_half == yl

    @pl.when(plane_self)
    def _():
        pltpu.make_async_copy(xt.at[:, pl.ds(40 * k, 40)], XZ.at[yl, tile], zr.at[yl, tile]).start()

    def c_core():
        return remote(CB.at[yl, k], CB.at[yl, k], cs.at[0], cr.at[0], core)

    def c_across():
        return remote(CB.at[yl, k], CB.at[yl, k], cs.at[1], cr.at[1], across)

    def c_relay():
        return remote(CB.at[1 - yl, k], CB.at[1 - yl, k], cs.at[2], cr.at[2], core)

    pick_slot = jnp.maximum(list_slot(0), list_slot(1)) + 1
    c_slot = pick_slot + C_READY

    def rows_of(ids):
        hit = lax.broadcasted_iota(jnp.int32, (512, 256), 0).astype(F32) == ids
        return jnp.where(hit, 1.0, 0.0).astype(BF16)

    def pick():
        take_anc.wait()
        own = rows_of(lst[0:1, :])
        hits = [rows_of(LB[jj, 0:1, :]) for jj in range(2)]
        block = AV[...]
        high, mid = split(block)
        rest = ((block - high.astype(F32)) - mid.astype(F32)).astype(BF16)
        found = []
        for part in (high, mid, rest):
            kept = lax.dot_general(own, part, (((0,), (0,)), ((), ())), preferred_element_type=F32).astype(BF16)
            found.append([
                jnp.dot(kept[:, 512 * jj : 512 * jj + 512], hits[jj], preferred_element_type=F32) for jj in range(2)
            ])
        for jj in range(2):
            CB[yl, k, jj] = found[0][jj] + (found[1][jj] + found[2][jj])
        c_across().start()
        c_core().start()

    def c_arrived():
        c_core().wait_recv()
        c_relay().wait_recv()
        for yb in range(2):
            for j in range(4):
                high, low = split(CB[yb, j // 2, j % 2])
                CH[yb, j], CL[yb, j] = high, low

    def peer(w, yb):
        turn = lax.rem(8 - w, 8)
        x, y = lax.rem(lax.div(p, 2) + lax.rem(turn, 4), 4), lax.rem(p + lax.div(turn, 4), 2)
        return remote(PB.at[w, yb], RB.at[w, yb], ds.at[w, yb], dr.at[w, yb], (r, 4 * x + 2 * y + k))

    def multiply(w):
        pieces = [stack(XR[j, w]) for j in range(4)]
        for yb in range(2):
            total = jnp.zeros((80, 256), F32)
            for j in range(4):
                total = total + dot3(pieces[j], (CH[yb, j], CL[yb, j]))
            PB[w, yb] = total

            @pl.when(w > 0)
            def _():
                peer(w, yb).start()

    first_multiply = jnp.maximum(PARTS + 3 + HOP * behind(3), c_slot)

    @pl.loop(0, GROUPS)
    def _(g):
        for jj in range(2):

            @pl.when((g > 0) & (list_slot(jj) == g))
            def _():
                list_step(jj)

        for i in range(4):
            forward(g, i)

        pl.when(g == pick_slot)(pick)

        @pl.when(g == pick_slot + C_RELAY)
        def _():
            c_across().wait_recv()
            c_relay().start()

        @pl.when((g >= 1) & (g <= 16) & jnp.logical_not(plane_self & (g == 1)))
        def _():
            plane_send(g - 1).start()

        pl.when(g == c_slot)(c_arrived)
        ready = g - first_multiply

        @pl.when((ready >= 0) & (ready < 8 * PARTS) & (lax.rem(jnp.maximum(ready, 0), PARTS) == 0))
        def _():
            multiply(lax.div(ready, PARTS))

    def s_copies(yb):
        own, other = SG.at[k, yl, yb], SG.at[k, 1 - yl, yb]
        return (
            remote(own, own, ss.at[0, yb], sr.at[0, yb], across),
            remote(own, own, ss.at[1, yb], sr.at[1, yb], core),
            remote(other, other, ss.at[2, yb], sr.at[2, yb], core),
        )

    for yb in range(2):
        total = PB[0, yb]
        for w in range(1, 8):
            peer(w, yb).wait_recv()
            total = total + RB[w, yb]
        SG[k, yl, yb] = -total
        for copy in s_copies(yb)[:2]:
            copy.start()
    for yb in range(2):
        s_copies(yb)[0].wait_recv()
        s_copies(yb)[2].start()
    so[...] = SG[k, :, yl, :, 0:240]

    for i in range(16):
        pltpu.make_async_copy(xt.at[:, pl.ds(0, 40)], XZ.at[i // 8, i % 8], zr.at[i // 8, i % 8]).wait()
    for yb in range(2):
        for copy in s_copies(yb)[1:]:
            copy.wait_recv()
        side = split(SG[:, :, yb].reshape(320, 256))

        @pl.loop(0, 2)
        def _(half):
            part = pl.ds(8 * half, 8)
            total = dot3(stack(XZ[yb, pl.ds(4 * half, 4)].reshape(320, 256)), side).reshape(8, 40, 320)
            tp[part, :, 0:320] = total + tp[part, :, 0:320] if yb else total

    def fold(way, step, part):
        rows = pl.ds(*FOLDS[part])
        there = at_z(-5 if way else 5) if step == 7 else (down if way else up)
        return remote(
            FS.at[way, step, rows], FR.at[way, step, rows], fs.at[way, step, part], fr.at[way, step, part], there
        )

    def fold_send(way, step, before, distance, part):
        rows = pl.ds(*FOLDS[part])
        mine = tp[lax.rem(z + (Z - distance if way else distance), Z), rows]
        if before is not None:
            fold(way, before, part).wait_recv()
            mine = mine + FR[way, before, rows]
        FS[way, step, rows] = mine
        fold(way, step, part).start()

    for step in range(4):
        for part in range(len(FOLDS)):
            for way in range(2):
                last = 2 + way
                if step < last:
                    fold_send(way, 4 + step, 3 + step if step else None, 7 + way - step, part)
                elif step == last:
                    fold_send(way, 7, 3 + step, 5, part)
        for part in range(len(FOLDS)):
            for way in range(2):
                fold_send(way, step, step - 1 if step else None, 4 - step, part)
    for part in range(len(FOLDS)):
        for way in range(2):
            fold(way, 3, part).wait_recv()
            fold(way, 7, part).wait_recv()
    PX[0] = tp[z] + (FR[0, 3] + FR[1, 3]) + (FR[0, 7] + FR[1, 7])
    swap = remote(PX.at[0], PX.at[1], px.at[0], px.at[1], core)
    swap.start()
    swap.wait_recv()
    own, other = PX[0], PX[1]
    own = jnp.where(k == 0, own[:, 0:160], own[:, 160:320])
    other = jnp.where(k == 0, other[:, 0:160], other[:, 160:320])
    diag[0:40, :] = jnp.where(k == 0, own, other)
    diag[40:80, :] = jnp.where(k == 0, other, own)
    swap.wait_send()
    for step in range(8):
        for part in range(len(FOLDS)):
            fold(1, step, part).wait_send()
            if step != 6:
                fold(0, step, part).wait_send()

    for jj in range(2):
        for copy, wanted in list_sends(jj):
            pl.when(wanted)(copy.wait_send)
    for h in range(2):
        for part in range(PARTS):
            pl.when(jnp.logical_not(own_local(h)))(own_send(h, part).wait_send)

    @pl.loop(0, 16)
    def _(n):
        pl.when(jnp.logical_not(plane_self & (n == 0)))(plane_send(n).wait_send)

    for i in range(4):

        @pl.when(behind(i) + i < 15)
        def _():
            @pl.loop(0, 8 * PARTS)
            def _(n):
                ring(line_block(i), n).wait_send()

    for copy in (c_core(), c_across(), c_relay(), *s_copies(0), *s_copies(1)):
        copy.wait_send()

    @pl.loop(1, 8)
    def _(w):
        peer(w, 0).wait_send()
        peer(w, 1).wait_send()


def shards(anc_inverse, panel, local_rows, inv_diag):
    vmem = pl.BlockSpec(memory_space=pltpu.VMEM)
    dma = pltpu.SemaphoreType.DMA
    so, folded = pl.pallas_call(
        panel_kernel,
        out_shape=(
            jax.ShapeDtypeStruct((2, 80, 240), F32),
            jax.ShapeDtypeStruct(inv_diag.shape, F32),
        ),
        in_specs=[pl.BlockSpec(memory_space=pl.ANY), vmem, vmem],
        out_specs=(vmem, vmem),
        scratch_shapes=[
            pltpu.VMEM((512, 1024), F32),
            pltpu.VMEM((2, 80, 256), F32),
            pltpu.VMEM((8, 256), F32),
            pltpu.VMEM((4, 8, 80, 256), F32),
            pltpu.VMEM((2, 8, 256), F32),
            pltpu.VMEM((2, 2, 2, 256, 256), F32),
            pltpu.VMEM((2, 4, 256, 256), BF16),
            pltpu.VMEM((2, 4, 256, 256), BF16),
            pltpu.VMEM((8, 2, 80, 256), F32),
            pltpu.VMEM((8, 2, 80, 256), F32),
            pltpu.VMEM((2, 2, 2, 80, 256), F32),
            pltpu.VMEM((2, 8, 2, 40, 256), F32),
            pltpu.VMEM((Z, 40, 384), F32),
            pltpu.VMEM((2, 8, 40, 384), F32),
            pltpu.VMEM((2, 8, 40, 384), F32),
            pltpu.VMEM((2, 40, 384), F32),
            dma((4, 8 * PARTS)), dma((4, 8 * PARTS)),
            dma((2, PARTS)),
            dma((2, 3)), dma((2,)),
            dma((3,)), dma((3,)),
            dma((8, 2)), dma((8, 2)),
            dma((3, 2)), dma((3, 2)),
            dma((16,)), dma((2, 8)),
            dma, dma((2, 8, 2)), dma((2, 8, 2)), dma((2,)),
        ],
        compiler_params=pltpu.CompilerParams(collective_id=0, has_side_effects=True),
        name="panel_products",
    )(anc_inverse, panel.T, local_rows.reshape(1, -1))
    sigma_diag = inv_diag - folded
    sigma_off = so.reshape(160, 240).T
    return (sigma_off, sigma_diag)


def solution(mesh):
    placed = (P("row", "col"), P("row", "col"), P("row"), P("row", "col"))
    return jax.shard_map(
        shards,
        mesh=mesh,
        in_specs=placed,
        out_specs=(P("row", "col"), P("row", "col")),
        check_vma=False,
    )
```

time: 166 us -> 158 us (0.952)
  the two profiles are of different devices: /device:TPU:21 before, /device:TPU:7 now
where the time goes in v3:
time: 158 us
  Pallas kernels  154 us (97%)
  local copies, waits for them, and re-layouts  1.6 us (1%)
    pallas_call x1, Pallas kernels, shards(): pl.pallas_call(panel_kernel, out_shape=(jax.ShapeDtypeStruct((2, 80, 240)...  154 us

profile of v3, /device:TPU:7, one launch (start us, length us, event | category | flops | bytes accessed | tf_op | source)
XLA Modules:
  0.0 157.7 jit_solution(9181194150437698529)
XLA Ops:
  0.6 0.0 copy-start
  0.6 153.9 %panel_products.1 = (f32[2,80,240]{2,1,0:T(8,128)}, f32[80,160]{1,0:T(8,128)}) custom-call(f32[512,1024]{1,0:T(8,128)} %anc.1, f32[160,240]{1,0:T(8,128)} %bitcast.5, s32[1,240]{1,0:T(1,128)} %bitcast.7), custom_call_target="tpu_custom_call" | custom-call | tf_op jit(solution)/shard_map/panel_products/pallas_call | solution.py:387
  154.6 0.0 copy-done
  154.6 1.5 sub.3
  156.1 1.6 %copy.7 = f32[240,160]{0,1:T(8,128)} copy(f32[240,160]{0,1:T(8,128)} %bitcast.6) | data formatting | bytes 307200
Async XLA Ops:
  0.6 153.9 %copy-start = (f32[80,160]{1,0:T(8,128)S(1)}, f32[80,160]{1,0:T(8,128)}, u32[]{:S(2)}) copy-start(f32[80,160]{1,0:T(8,128)} %param.7) | copy-start | bytes 153604

commit v4 on v3

--- a/solution.py
+++ b/solution.py
@@ -9,12 +9,10 @@
 
 MESH = pl.DeviceIdType.MESH
 Z = 16
-PARTS = 1
-PIECE = 80 // PARTS
 HOP = 1
 C_RELAY = 4
 C_READY = 6
-GROUPS = max(8 * PARTS + 3 + 12 * HOP, 10 + C_READY + 7 * PARTS) + 2
+GROUPS = max(9 + 3 + 12 * HOP, 10 + C_READY + 9) + 2
 FOLDS = ((0, 24), (24, 16))
 F32 = jnp.float32
 BF16 = jnp.bfloat16
@@ -48,7 +46,7 @@
 def panel_kernel(
     anc, panel, ids, so, diag,
     AV, xt, lst, XR, LB, CB, CH, CL, PB, RB, SG, XZ, tp, FS, FR, PX,
-    xs, xr, asend, ls, lr, cs, cr, ds, dr, ss, sr, zs, zr, av, fs, fr, px,
+    xs, hs, xr, asend, ls, lr, cs, cr, ds, dr, ss, sr, zs, zr, av, fs, fr, px,
 ):
     r, c = lax.axis_index("row"), lax.axis_index("col")
     yl, z = lax.div(r, Z), lax.rem(r, Z)
@@ -114,13 +112,15 @@
     turn = 4 * lax.rem(p + to_p, 2) + lax.rem(lax.div(p, 2) - lax.div(to_p, 2) + 4, 4)
     own_n = lax.rem(8 - turn, 8)
 
-    def own_pair(h, part):
-        there = XR.at[to_j, own_n, pl.ds(PIECE * part, PIECE)]
-        return xt.at[h, pl.ds(PIECE * part, PIECE)], there, xr.at[to_j, PARTS * own_n + part]
-
-    def own_send(h, part):
-        src, dst, sem = own_pair(h, part)
-        return remote(src, dst, asend.at[h, part], sem, (Z * h + z, 2 * to_p + k))
+    lent = (k == 0) & (own_n == 7)
+    own_at = jnp.where(k == 1, own_n + jnp.minimum(own_n, 1), jnp.where(lent, 1, own_n))
+
+    def own_pair(h):
+        return xt.at[h], XR.at[to_j, own_at], xr.at[to_j, own_at]
+
+    def own_send(h):
+        src, dst, sem = own_pair(h)
+        return remote(src, dst, asend.at[h], sem, (Z * h + z, 2 * to_p + jnp.where(lent, 1, k)))
 
     def own_local(h):
         return (to_p == p) & (yl == h)
@@ -131,26 +131,28 @@
         def _():
             list_step(jj)
 
-    for part in range(PARTS):
-        for h in range(2):
-
-            @pl.when(own_local(h))
-            def _():
-                pltpu.make_async_copy(*own_pair(h, part)).start()
-
-            @pl.when(jnp.logical_not(own_local(h)))
-            def _():
-                own_send(h, part).start()
+    for h in range(2):
+
+        @pl.when(own_local(h))
+        def _():
+            pltpu.make_async_copy(*own_pair(h)).start()
+
+        @pl.when(jnp.logical_not(own_local(h)))
+        def _():
+            own_send(h).start()
 
     base = lax.rem(4 * p, Z)
     place = jnp.where(k == 0, lax.rem(z - base + Z, Z), lax.rem(base + 3 - z + Z, Z))
     low, late = jnp.minimum(place, 3), jnp.maximum(place - 3, 0)
     onward = at_z(1 - 2 * k)
 
+    pieces_here = 7 + 2 * k
+
     def ring(j, n):
-        w, part = lax.div(n, PARTS), lax.rem(n, PARTS)
-        piece = XR.at[j, w, pl.ds(PIECE * part, PIECE)]
-        return remote(piece, piece, xs.at[j, n], xr.at[j, n], onward)
+        return remote(XR.at[j, n], XR.at[j, n], xs.at[j, n], xr.at[j, n], onward)
+
+    def hand_over(j):
+        return remote(XR.at[j, 1], XR.at[j, 7], hs.at[j], xr.at[j, 7], core)
 
     def behind(i):
         return jnp.where(i <= low, late, 12)
@@ -162,11 +164,13 @@
     def forward(g, i):
         n = g - HOP * behind(i) - i
 
-        @pl.when((n >= 0) & (n < 8 * PARTS))
-        def _():
-            copy = ring(line_block(i), jnp.maximum(n, 0))
+        @pl.when((n >= 0) & (n < pieces_here))
+        def _():
+            j = line_block(i)
+            copy = ring(j, jnp.maximum(n, 0))
             copy.wait_recv()
             pl.when(behind(i) + i < 15)(copy.start)
+            pl.when((k == 1) & (n == 1))(hand_over(j).start)
 
     tile, tile_half = lax.rem(c, 8), lax.div(c, 8)
 
@@ -230,7 +234,8 @@
         return remote(PB.at[w, yb], RB.at[w, yb], ds.at[w, yb], dr.at[w, yb], (r, 4 * x + 2 * y + k))
 
     def multiply(w):
-        pieces = [stack(XR[j, w]) for j in range(4)]
+        at = jnp.where(k == 1, w + jnp.minimum(w, 1), w)
+        pieces = [stack(XR[j, at]) for j in range(4)]
         for yb in range(2):
             total = jnp.zeros((80, 256), F32)
             for j in range(4):
@@ -241,7 +246,7 @@
             def _():
                 peer(w, yb).start()
 
-    first_multiply = jnp.maximum(PARTS + 3 + HOP * behind(3), c_slot)
+    first_multiply = jnp.maximum(1 + 3 + HOP * behind(3), c_slot)
 
     @pl.loop(0, GROUPS)
     def _(g):
@@ -268,9 +273,15 @@
         pl.when(g == c_slot)(c_arrived)
         ready = g - first_multiply
 
-        @pl.when((ready >= 0) & (ready < 8 * PARTS) & (lax.rem(jnp.maximum(ready, 0), PARTS) == 0))
-        def _():
-            multiply(lax.div(ready, PARTS))
+        @pl.when((ready >= 0) & (ready < pieces_here) & ((k == 0) | (ready != 1)))
+        def _():
+            multiply(jnp.maximum(ready - jnp.where(ready > 1, k, 0), 0))
+
+    @pl.when(k == 0)
+    def _():
+        for j in range(4):
+            ring(j, 7).wait_recv()
+        multiply(7)
 
     def s_copies(yb):
         own, other = SG.at[k, yl, yb], SG.at[k, 1 - yl, yb]
@@ -357,8 +368,7 @@
         for copy, wanted in list_sends(jj):
             pl.when(wanted)(copy.wait_send)
     for h in range(2):
-        for part in range(PARTS):
-            pl.when(jnp.logical_not(own_local(h)))(own_send(h, part).wait_send)
+        pl.when(jnp.logical_not(own_local(h)))(own_send(h).wait_send)
 
     @pl.loop(0, 16)
     def _(n):
@@ -368,9 +378,12 @@
 
         @pl.when(behind(i) + i < 15)
         def _():
-            @pl.loop(0, 8 * PARTS)
+            @pl.loop(0, pieces_here)
             def _(n):
                 ring(line_block(i), n).wait_send()
+
+    for j in range(4):
+        pl.when(k == 1)(hand_over(j).wait_send)
 
     for copy in (c_core(), c_across(), c_relay(), *s_copies(0), *s_copies(1)):
         copy.wait_send()
@@ -396,7 +409,7 @@
             pltpu.VMEM((512, 1024), F32),
             pltpu.VMEM((2, 80, 256), F32),
             pltpu.VMEM((8, 256), F32),
-            pltpu.VMEM((4, 8, 80, 256), F32),
+            pltpu.VMEM((4, 9, 80, 256), F32),
             pltpu.VMEM((2, 8, 256), F32),
             pltpu.VMEM((2, 2, 2, 256, 256), F32),
             pltpu.VMEM((2, 4, 256, 256), BF16),
@@ -409,8 +422,8 @@
             pltpu.VMEM((2, 8, 40, 384), F32),
             pltpu.VMEM((2, 8, 40, 384), F32),
             pltpu.VMEM((2, 40, 384), F32),
-            dma((4, 8 * PARTS)), dma((4, 8 * PARTS)),
-            dma((2, PARTS)),
+            dma((4, 9)), dma((4,)), dma((4, 9)),
+            dma((2,)),
             dma((2, 3)), dma((2,)),
             dma((3,)), dma((3,)),
             dma((8, 2)), dma((8, 2)),

time: 158 us -> 154 us (0.975)
  Pallas kernels: 154 us -> 149 us
    pallas_call x1, Pallas kernels: 154 us -> 149 us  [shards(): pl.pallas_call(panel_kernel, out_shape=(jax.ShapeDtypeStruct((2, 80, 240)...]
where the time goes in v4:
time: 154 us; the launch traced here: 153 us
  Pallas kernels  149 us (97%)
  local copies, waits for them, and re-layouts  1.6 us (1%)
    pallas_call x1, Pallas kernels, shards(): pl.pallas_call(panel_kernel, out_shape=(jax.ShapeDtypeStruct((2, 80, 240)...  149 us

profile of v4, /device:TPU:7, one launch (start us, length us, event | category | flops | bytes accessed | tf_op | source)
XLA Modules:
  0.0 152.8 jit_solution(14084943679273912841)
XLA Ops:
  0.6 0.0 copy-start
  0.6 149.1 %panel_products.1 = (f32[2,80,240]{2,1,0:T(8,128)}, f32[80,160]{1,0:T(8,128)}) custom-call(f32[512,1024]{1,0:T(8,128)} %anc.1, f32[160,240]{1,0:T(8,128)} %bitcast.5, s32[1,240]{1,0:T(1,128)} %bitcast.7), custom_call_target="tpu_custom_call" | custom-call | tf_op jit(solution)/shard_map/panel_products/pallas_call | solution.py:400
  149.7 0.0 copy-done
  149.7 1.5 %sub.3 = f32[80,160]{1,0:T(8,128)} subtract(f32[80,160]{1,0:T(8,128)S(1)} %copy-done, f32[80,160]{1,0:T(8,128)} %get-tuple-element.5) | non-fusion elementwise | flops 12800 | bytes 153600 | tf_op jit(solution)/shard_map/sub | solution.py:437
  151.3 1.6 %copy.7 = f32[240,160]{0,1:T(8,128)} copy(f32[240,160]{0,1:T(8,128)} %bitcast.6) | data formatting | bytes 307200
Async XLA Ops:
  0.6 149.1 %copy-start = (f32[80,160]{1,0:T(8,128)S(1)}, f32[80,160]{1,0:T(8,128)}, u32[]{:S(2)}) copy-start(f32[80,160]{1,0:T(8,128)} %param.7) | copy-start | bytes 153604

commit v5 on v4

--- a/solution.py
+++ b/solution.py
@@ -266,9 +266,12 @@
             c_across().wait_recv()
             c_relay().start()
 
-        @pl.when((g >= 1) & (g <= 16) & jnp.logical_not(plane_self & (g == 1)))
-        def _():
-            plane_send(g - 1).start()
+        due = g - HOP * late - 1
+
+        @pl.when((due >= 0) & (due < 8))
+        def _():
+            pl.when(jnp.logical_not(plane_self & (due == 0)))(plane_send(2 * due).start)
+            plane_send(2 * due + 1).start()
 
         pl.when(g == c_slot)(c_arrived)
         ready = g - first_multiply

time: 154 us -> 151 us (0.981)
  Pallas kernels: 149 us -> 146 us
    pallas_call x1, Pallas kernels: 149 us -> 146 us  [shards(): pl.pallas_call(panel_kernel, out_shape=(jax.ShapeDtypeStruct((2, 80, 240)...]
where the time goes in v5:
time: 151 us; the launch traced here: 150 us
  Pallas kernels  146 us (97%)
  local copies, waits for them, and re-layouts  1.6 us (1%)
  other arithmetic  1.53 us (1%)
    pallas_call x1, Pallas kernels, shards(): pl.pallas_call(panel_kernel, out_shape=(jax.ShapeDtypeStruct((2, 80, 240)...  146 us

profile of v5, /device:TPU:7, one launch (start us, length us, event | category | flops | bytes accessed | tf_op | source)
XLA Modules:
  0.0 149.7 jit_solution(14059470382297713609)
XLA Ops:
  0.6 0.0 copy-start
  0.6 145.9 %panel_products.1 = (f32[2,80,240]{2,1,0:T(8,128)}, f32[80,160]{1,0:T(8,128)}) custom-call(f32[512,1024]{1,0:T(8,128)} %anc.1, f32[160,240]{1,0:T(8,128)} %bitcast.5, s32[1,240]{1,0:T(1,128)} %bitcast.7), custom_call_target="tpu_custom_call" | custom-call | tf_op jit(solution)/shard_map/panel_products/pallas_call | solution.py:403
  146.6 0.0 copy-done
  146.6 1.5 %sub.3 = f32[80,160]{1,0:T(8,128)} subtract(f32[80,160]{1,0:T(8,128)S(1)} %copy-done, f32[80,160]{1,0:T(8,128)} %get-tuple-element.5) | non-fusion elementwise | flops 12800 | bytes 153600 | tf_op jit(solution)/shard_map/sub | solution.py:440
  148.1 1.6 %copy.7 = f32[240,160]{0,1:T(8,128)} copy(f32[240,160]{0,1:T(8,128)} %bitcast.6) | data formatting | bytes 307200
Async XLA Ops:
  0.6 145.9 %copy-start = (f32[80,160]{1,0:T(8,128)S(1)}, f32[80,160]{1,0:T(8,128)}, u32[]{:S(2)}) copy-start(f32[80,160]{1,0:T(8,128)} %param.7) | copy-start | bytes 153604
